TPU v7x, 32 devices: a whole 2x2x4 slice. The times are simulated.
32 devices in a mesh: group: 2 (over y), slab: 4 (over z), subj: 2 (over x), yslab: 2 (over core).
Axes of the slice: x: 2, y: 2, z: 4, core: 2. Of those that a mesh axis runs over, the one named last changes fastest.
Arguments:
- subjects: bfloat16 [4, 64, 16, 256], P(('group', 'subj'), 'slab', 'yslab'), parts along dimension 0, may hold values from -6 to 6
- offsets: int32 [4, 3, 64, 16, 256], P(('group', 'subj'), None, 'slab', 'yslab'), parts along dimension 0, may hold values from -2 to 1
- template: float32 [128, 16, 256], P(('group', 'slab'), 'yslab'), parts along dimension 0, may hold values from -6 to 6
- control: float32 [4, 3, 19, 7, 128], P(('group', 'subj')), parts along dimension 0, may hold values from -8 to 8
Outputs:
- template_out: float32 [128, 16, 256], P(('group', 'slab'), 'yslab'), parts along dimension 0
- control_out: float32 [4, 3, 19, 7, 128], P(('group', 'subj')), parts along dimension 0
There are 2 independent parts, one for each index of `group`. A program takes and returns all parts, laid end to end along the dimension named above; each array names one. Nothing has to cross between parts.
All inputs are finite; a program needn't handle non-finite values.
Results may differ from a plain program's by a relative error of at most 0.00065.
Values may be sent and summed in bfloat16 or wider, within the bound.
A program may use at most 64 MiB of HBM per device.

v0:
```python
import jax
import jax.numpy as jnp
from jax import lax
from jax.sharding import PartitionSpec as P

KNOT = 4
KNOT_X = 2
HALO = 2
ITERS = 2
step_length = 0.5
tiny_term = 1e-06


def extended_2(value, sides, width):
    for axis, dim in sides:
        peers, length = (lax.axis_size(axis), value.shape[dim])
        up = [(i, (i + 1) % peers) for i in range(peers - 1)]
        down = [(j, i) for i, j in up]
        last = lax.slice_in_dim(value, length - width, length, axis=dim)
        initial = lax.slice_in_dim(value, 0, width, axis=dim)
        before = lax.ppermute(last, axis, up)
        after = lax.ppermute(initial, axis, down)
        value = jnp.concatenate([before, value, after], axis=dim)
    return value


def shifted(block, axis, distance):
    devices = range(lax.axis_size(axis))
    route = [(i - distance, i) for i in devices if i - distance in devices]
    return lax.ppermute(block, axis, route)


def from_root(value, axis, source):
    kept = jnp.where(lax.axis_index(axis) == source, value, 0).astype(value.dtype)
    return lax.psum(kept, axis)


def basis(positions, columns, spacing, wrap):
    cell = positions // spacing
    frac = (positions - cell * spacing).astype(jnp.float32) / spacing
    weights = [
        (1.0 - frac) ** 3 / 6.0,
        (3.0 * frac**3 - 6.0 * frac**2 + 4.0) / 6.0,
        (-3.0 * frac**3 + 3.0 * frac**2 + 3.0 * frac + 1.0) / 6.0,
        frac**3 / 6.0,
    ]
    index = jnp.arange(columns, dtype=jnp.int32)
    matrix = jnp.zeros((positions.shape[0], columns), jnp.float32)
    for offset in range(4):
        target = cell + offset
        if wrap:
            target = target % columns
        matrix = matrix + jnp.where(
            index[None, :] == target[:, None], weights[offset][:, None], 0.0
        )
    return matrix


def forward_field(coeffs, basis_z, basis_y, basis_x):
    high = lax.Precision.HIGHEST
    first = jnp.einsum("cabg,za->czbg", coeffs, basis_z, precision=high)
    second = jnp.einsum("czbg,yb->czyg", first, basis_y, precision=high)
    return jnp.einsum("czyg,xg->czyx", second, basis_x, precision=high)


def adjoint_field(gradient, basis_z, basis_y, basis_x):
    high = lax.Precision.HIGHEST
    first = jnp.einsum("czyx,xg->czyg", gradient, basis_x, precision=high)
    second = jnp.einsum("czyg,yb->czbg", first, basis_y, precision=high)
    return jnp.einsum("czbg,za->cabg", second, basis_z, precision=high)


def choose(shift_of, table, lead):
    result = table[-HALO + lead]
    for value in range(-HALO + 1, HALO):
        result = jnp.where(shift_of == value, table[value + lead], result)
    return result


def trilinear_local(volume, shifts, fraction, depth, height, width):
    frac_z, frac_y, frac_x = (fraction[0], fraction[1], fraction[2])
    shift_z, shift_y, shift_x = (shifts[0], shifts[1], shifts[2])
    along_y_of = {}
    diff_y_of = {}
    diff_xy_of = {}
    for move_z in range(-HALO, HALO + 1):
        along_x_of = {}
        diff_x_of = {}
        for move_y in range(-HALO, HALO + 1):
            plane = volume[
                move_z + HALO : move_z + HALO + depth, move_y + HALO : move_y + HALO + height, :
            ].astype(jnp.float32)
            columns = {}
            for move_x in range(-HALO, HALO + 1):
                columns[move_x] = plane[:, :, move_x + HALO : move_x + HALO + width]
            low = choose(shift_x, columns, 0)
            high = choose(shift_x, columns, 1)
            along_x_of[move_y] = low * (1.0 - frac_x) + high * frac_x
            diff_x_of[move_y] = high - low
        along_low = choose(shift_y, along_x_of, 0)
        along_high = choose(shift_y, along_x_of, 1)
        diff_low = choose(shift_y, diff_x_of, 0)
        diff_high = choose(shift_y, diff_x_of, 1)
        along_y_of[move_z] = along_low * (1.0 - frac_y) + along_high * frac_y
        diff_y_of[move_z] = along_high - along_low
        diff_xy_of[move_z] = diff_low * (1.0 - frac_y) + diff_high * frac_y
    along_y = [choose(shift_z, along_y_of, 0), choose(shift_z, along_y_of, 1)]
    diff_y = [choose(shift_z, diff_y_of, 0), choose(shift_z, diff_y_of, 1)]
    diff_xy = [choose(shift_z, diff_xy_of, 0), choose(shift_z, diff_xy_of, 1)]
    warped = along_y[0] * (1.0 - frac_z) + along_y[1] * frac_z
    slope_z = along_y[1] - along_y[0]
    slope_y = diff_y[0] * (1.0 - frac_z) + diff_y[1] * frac_z
    slope_x = diff_xy[0] * (1.0 - frac_z) + diff_xy[1] * frac_z
    return (warped, jnp.stack([slope_z, slope_y, slope_x]))


def shards(subjects, offsets, template, control):
    local_subjects = subjects.shape[0]
    depth, height, width = (subjects.shape[1], subjects.shape[2], subjects.shape[3])
    rows_slab = depth // KNOT
    cohort = local_subjects * lax.axis_size("subj")
    extended = extended_2(subjects, (("slab", 1), ("yslab", 2)), HALO)
    extended = jnp.pad(extended, ((0, 0), (0, 0), (0, 0), (HALO, HALO)))
    basis_z = basis(jnp.arange(depth, dtype=jnp.int32), rows_slab + 3, KNOT, False)
    y_start = lax.axis_index("yslab") * height
    basis_y = basis(y_start + jnp.arange(height, dtype=jnp.int32), control.shape[3], KNOT, False)
    basis_x = basis(jnp.arange(width, dtype=jnp.int32), control.shape[4], KNOT_X, True)
    first_row = lax.axis_index("slab") * rows_slab
    current = template
    coeffs_all = control
    for iteration in range(ITERS):
        band_coeffs = lax.dynamic_slice_in_dim(coeffs_all[0], first_row, rows_slab + 3, 1)
        displace = forward_field(band_coeffs, basis_z, basis_y, basis_x)
        tanh_u = jnp.tanh(displace)
        fraction = 0.5 + 0.5 * tanh_u
        warped, slopes = trilinear_local(extended[0], offsets[0], fraction, depth, height, width)
        resid = warped - current
        grad_u = resid[None] * slopes * (1.0 - tanh_u * tanh_u)
        band_list = [adjoint_field(grad_u, basis_z, basis_y, basis_x)]
        band_grid = jnp.stack(band_list)
        current = lax.psum(warped, "subj") / cohort
        band_grid = lax.psum(band_grid.astype(jnp.bfloat16), "yslab").astype(jnp.float32)
        head_rows = band_grid[:, :, :rows_slab]
        tail_part = band_grid[:, :, rows_slab:]
        carried = shifted(tail_part, "slab", 1)
        head_rows = head_rows.at[:, :, :3].add(carried)
        owned = lax.all_gather(head_rows.astype(jnp.bfloat16), "slab", axis=2, tiled=True).astype(
            head_rows.dtype
        )
        last_part = from_root(tail_part, "slab", lax.axis_size("slab") - 1)
        grid = jnp.concatenate([owned, last_part], axis=2)
        lengths = jnp.sqrt(jnp.sum(grid * grid, axis=1))
        peak = jnp.max(lengths, axis=(1, 2, 3))
        coeffs_all = coeffs_all - step_length * grid / (peak[:, None, None, None, None] + tiny_term)
    return (current, coeffs_all)


def solution(mesh):
    in_specs = (
        P(("group", "subj"), "slab", "yslab", None),
        P(("group", "subj"), None, "slab", "yslab", None),
        P(("group", "slab"), "yslab", None),
        P(("group", "subj"), None, None, None, None),
    )
    out_specs = (P(("group", "slab"), "yslab", None), P(("group", "subj"), None, None, None, None))
    return jax.shard_map(shards, mesh=mesh, in_specs=in_specs, out_specs=out_specs, check_vma=False)
```

profile of v0, /device:TPU:0, one launch (start us, length us, event | category | flops | bytes accessed | tf_op | source)
XLA Modules:
  0.0 160.3 jit_solution(13082636263804256856)
XLA Ops:
  7.9 1.3 collective-permute-start.1
  9.2 5.6 %collective-permute-start = (bf16[1,2,8,256]{3,2,1,0:T(8,128)(2,1)S(1)}, bf16[1,2,8,256]{3,2,1,0:T(8,128)(2,1)S(1)}, u32[]{:S(2)}, u32[]{:S(2)}) collective-permute-start(bf16[1,2,8,256]{3,2,1,0:T(8,128)(2,1)S(1)} %get-tuple-element.162), channel_id=1, source_target_pairs={{0,4},{4,8},{8,12},{1,5},{5,9},{9,13},{2,6},{6,10},{10,14},{3,7},{... | collective-permute-start | bytes 24584 | tf_op jit(solution)/shard_map/ppermute | solution.py:21
  15.2 0.9 constant_dynamic-slice_fusion
  17.6 1.5 collective-permute-start.2
  19.0 1.3 collective-permute-start.3
  20.4 1.5 multiply_add_fusion.1
  25.5 3.3 %fusion.335 = (f32[16,8,256]{2,1,0:T(8,128)S(1)}, f32[16,8,256]{2,1,0:T(8,128)}, f32[16,8,256]{2,1,0:T(8,128)S(1)}, f32[16,8,256]{2,1,0:T(8,128)S(1)}, f32[16,8,...) fusion(f32[16,8,256]{2,1,0:T(8,128)S(1)} %copy-done.64, ...), kind=kLoop, calls=%fused_computation.598 | loop fusion | flops 8093696 | bytes 21266432 | tf_op jit(solution)/shard_map/sub | solution.py:137
  30.5 2.9 %add_bitcast_fusion.2 = (f32[1,16,8,256]{3,2,1,0:T(8,128)S(1)}, f32[16,8,256]{2,1,0:T(8,128)}, f32[16,8,256]{2,1,0:T(8,128)}, f32[16,8,256]{2,1,0:T(8,128)}, f32...) fusion(pred[1,1,16,8,256]{4,3,2,1,0:T(8,128)(4,1)S(1)} %get-tup, ...), kind=kLoop, calls=%fused_computation.248 | loop fusion | flops 2654208 | bytes 8454144 | tf_op jit(solution)/shard_map/stack | solution.py:114
  34.1 0.8 fusion.4
  35.9 4.2 %psum.42 = bf16[1,3,7,7,128]{4,2,3,1,0:T(8,128)(2,1)S(1)} all-reduce(bf16[1,3,7,7,128]{4,2,3,1,0:T(8,128)(2,1)S(1)} %fusion), channel_id=1, replica_groups=mesh['group'=2,'slab'=4,'subj'=2,'yslab'=2] {'yslab'}, use_global_device_ids=true, to_apply=%region_0.1 | all-reduce | flops 18816 | bytes 75264 | tf_op jit(solution)/shard_map/psum | solution.py:142
  40.8 3.8 %collective-permute-start.4 = (f32[1,3,3,7,128]{4,2,3,1,0:T(4,128)S(1)}, f32[1,3,3,7,128]{4,2,3,1,0:T(4,128)S(1)}, u32[]{:S(2)}, u32[]{:S(2)}) collective-permute-start(f32[1,3,3,7,128]{4,2,3,1,0:T(4,128)S(1)} %slice.1053), channel_id=1, source_target_pairs={{0,4},{4,8},{8,12},{1,5},{5,9},{9,13},{2,6},{6,10},{10,14},{3,7},{... | collective-permute-start | bytes 96776 | tf_op jit(solution)/shard_map/ppermute | solution.py:30
  44.6 17.6 %psum.43 = f32[1,3,3,7,128]{4,2,3,1,0:T(4,128)S(1)} all-reduce(f32[1,3,3,7,128]{4,2,3,1,0:T(4,128)S(1)} %broadcast_select_fusion.1), channel_id=1, replica_groups=mesh['group'=2,'slab'=4,'subj'=2,'yslab'=2] {'slab'}, use_global_device_ids=true, to_apply=%region_1.2 | all-reduce | flops 8064 | bytes 64512 | tf_op jit(solution)/shard_map/psum | solution.py:35
  63.2 13.4 %all_gather.6 = bf16[1,3,16,7,128]{4,3,1,0,2:T(8,128)(2,1)S(1)} all-gather(bf16[1,3,4,7,128]{4,3,1,0,2:T(8,128)(2,1)S(1)} %copy.8), channel_id=1, replica_groups=mesh['group'=2,'slab'=4,'subj'=2,'yslab'=2] {'slab'}, dimensions={2}, use_global_device_ids=true | all-gather | bytes 107520 | tf_op jit(solution)/shard_map/all_gather | solution.py:147
  78.1 1.1 copy_subtract_fusion
  80.2 1.5 multiply_add_fusion
  81.9 3.0 %subtract_bitcast_fusion = (f32[1,16,8,256]{3,2,1,0:T(8,128)}, f32[16,8,256]{2,1,0:T(8,128)S(1)}, f32[16,8,256]{2,1,0:T(8,128)S(1)}, f32[16,8,256]{2,1,0:T(8,128...) fusion(pred[1,1,16,8,256]{4,3,2,1,0:T(8,128)(4,1)S(1)} %get-tup, ...), kind=kLoop, calls=%fused_computation.191 | loop fusion | flops 4227072 | bytes 8716288 | tf_op jit(solution)/shard_map/stack | solution.py:114
  87.0 20.5 %all-reduce.4.cloned.1.call-done = (f32[16,8,256]{2,1,0:T(8,128)}, f32[16,8,256]{2,1,0:T(8,128)}) async-done(((f32[16,8,256]{2,1,0:T(8,128)}, f32[16,8,256]{2,1,0:T(8,128)}), (f32[16,8,256]{2,1,0:T(8,128)}, f32[16,8,256]{2,1,0:T(8,128)})) %all-reduce.4.cloned.1.call-update) | async-done | bytes 262160 | tf_op jit(solution)/shard_map/psum | solution.py:141
  107.5 0.9 multiply_subtract_fusion
  109.1 0.8 fusion.11
  111.0 3.5 %psum.46 = bf16[1,3,7,7,128]{4,2,3,1,0:T(8,128)(2,1)S(1)} all-reduce(bf16[1,3,7,7,128]{4,2,3,1,0:T(8,128)(2,1)S(1)} %fusion.1), channel_id=1, replica_groups=mesh['group'=2,'slab'=4,'subj'=2,'yslab'=2] {'yslab'}, use_global_device_ids=true, to_apply=%region_6.7 | all-reduce | flops 18816 | bytes 75264 | tf_op jit(solution)/shard_map/psum | solution.py:142
  116.1 3.4 %collective-permute-start.5 = (f32[1,3,3,7,128]{4,2,3,1,0:T(4,128)S(1)}, f32[1,3,3,7,128]{4,2,3,1,0:T(4,128)S(1)}, u32[]{:S(2)}, u32[]{:S(2)}) collective-permute-start(f32[1,3,3,7,128]{4,2,3,1,0:T(4,128)S(1)} %slice.1059), channel_id=1, source_target_pairs={{0,4},{4,8},{8,12},{1,5},{5,9},{9,13},{2,6},{6,10},{10,14},{3,7},{... | collective-permute-start | bytes 96776 | tf_op jit(solution)/shard_map/ppermute | solution.py:30
  119.5 17.6 %psum.47 = f32[1,3,3,7,128]{4,2,3,1,0:T(4,128)S(1)} all-reduce(f32[1,3,3,7,128]{4,2,3,1,0:T(4,128)S(1)} %broadcast_select_fusion), channel_id=1, replica_groups=mesh['group'=2,'slab'=4,'subj'=2,'yslab'=2] {'slab'}, use_global_device_ids=true, to_apply=%region_7.8 | all-reduce | flops 8064 | bytes 64512 | tf_op jit(solution)/shard_map/psum | solution.py:35
  138.0 13.2 %all_gather.7 = bf16[1,3,16,7,128]{4,3,1,0,2:T(8,128)(2,1)S(1)} all-gather(bf16[1,3,4,7,128]{4,3,1,0,2:T(8,128)(2,1)S(1)} %copy.12), channel_id=1, replica_groups=mesh['group'=2,'slab'=4,'subj'=2,'yslab'=2] {'slab'}, dimensions={2}, use_global_device_ids=true | all-gather | bytes 107520 | tf_op jit(solution)/shard_map/all_gather | solution.py:147
  152.6 0.9 copy.15
  (352 shorter events, 18.6 us)
Async XLA Ops:
  7.2 100.3 %all-reduce.4.cloned.1.call-start = ((), (), s32[]{:S(2)}) async-start(), calls=%async_computation | async-start | bytes 524288 | tf_op jit(solution)/shard_map/psum | solution.py:141
  7.9 9.6 %collective-permute-start.1 = (bf16[1,2,8,256]{3,2,1,0:T(8,128)(2,1)S(1)}, bf16[1,2,8,256]{3,2,1,0:T(8,128)(2,1)S(1)}, u32[]{:S(2)}, u32[]{:S(2)}) collective-permute-start(bf16[1,2,8,256]{3,2,1,0:T(8,128)(2,1)S(1)} %get-tuple-element.161), channel_id=1, source_target_pairs={{4,0},{8,4},{12,8},{5,1},{9,5},{13,9},{6,2},{10,6},{14,10},{7,3},{... | collective-permute-start | bytes 24584 | tf_op jit(solution)/shard_map/ppermute | solution.py:22
  9.2 7.9 %collective-permute-start = (bf16[1,2,8,256]{3,2,1,0:T(8,128)(2,1)S(1)}, bf16[1,2,8,256]{3,2,1,0:T(8,128)(2,1)S(1)}, u32[]{:S(2)}, u32[]{:S(2)}) collective-permute-start(bf16[1,2,8,256]{3,2,1,0:T(8,128)(2,1)S(1)} %get-tuple-element.162), channel_id=1, source_target_pairs={{0,4},{4,8},{8,12},{1,5},{5,9},{9,13},{2,6},{6,10},{10,14},{3,7},{... | collective-permute-start | bytes 24584 | tf_op jit(solution)/shard_map/ppermute | solution.py:21
  15.1 18.2 %copy-start.66 = (f32[256]{0:T(256)}, f32[256]{0:T(256)S(1)}, u32[]{:S(2)}) copy-start(f32[256]{0:T(256)S(1)} %get-tuple-element.189) | copy-start | bytes 3076
  15.2 5.2 %copy-start.69 = (s32[256]{0:T(256)}, s32[256]{0:T(256)S(1)}, u32[]{:S(2)}) copy-start(s32[256]{0:T(256)S(1)} %get-tuple-element.186) | copy-start | bytes 3076
  15.2 5.2 %copy-start.73 = (s32[256]{0:T(256)}, s32[256]{0:T(256)S(1)}, u32[]{:S(2)}) copy-start(s32[256]{0:T(256)S(1)} %get-tuple-element.187) | copy-start | bytes 3076
  17.1 3.3 %copy-start.77 = (s32[256]{0:T(256)}, s32[256]{0:T(256)S(1)}, u32[]{:S(2)}) copy-start(s32[256]{0:T(256)S(1)} %get-tuple-element.184) | copy-start | bytes 3076
  17.1 3.3 %copy-start.81 = (s32[256]{0:T(256)}, s32[256]{0:T(256)S(1)}, u32[]{:S(2)}) copy-start(s32[256]{0:T(256)S(1)} %get-tuple-element.185) | copy-start | bytes 3076
  17.6 4.3 %collective-permute-start.2 = (bf16[1,20,2,256]{3,2,1,0:T(2,128)(2,1)S(1)}, bf16[1,20,2,256]{3,2,1,0:T(2,128)(2,1)S(1)}, u32[]{:S(2)}, u32[]{:S(2)}) collective-permute-start(bf16[1,20,2,256]{3,2,1,0:T(2,128)(2,1)S(1)} %get-tuple-element.159), channel_id=1, source_target_pairs={{0,1},{2,3},{4,5},{6,7},{8,9},{10,11},{12,13},{14,15},{16,17},{18,... | collective-permute-start | bytes 61448 | tf_op jit(solution)/shard_map/ppermute | solution.py:21
  19.0 3.1 %collective-permute-start.3 = (bf16[1,20,2,256]{3,2,1,0:T(2,128)(2,1)S(1)}, bf16[1,20,2,256]{3,2,1,0:T(2,128)(2,1)S(1)}, u32[]{:S(2)}, u32[]{:S(2)}) collective-permute-start(bf16[1,20,2,256]{3,2,1,0:T(2,128)(2,1)S(1)} %get-tuple-element.160), channel_id=1, source_target_pairs={{1,0},{3,2},{5,4},{7,6},{9,8},{11,10},{13,12},{15,14},{17,16},{19,... | collective-permute-start | bytes 61448 | tf_op jit(solution)/shard_map/ppermute | solution.py:22
  40.8 21.4 %collective-permute-start.4 = (f32[1,3,3,7,128]{4,2,3,1,0:T(4,128)S(1)}, f32[1,3,3,7,128]{4,2,3,1,0:T(4,128)S(1)}, u32[]{:S(2)}, u32[]{:S(2)}) collective-permute-start(f32[1,3,3,7,128]{4,2,3,1,0:T(4,128)S(1)} %slice.1053), channel_id=1, source_target_pairs={{0,4},{4,8},{8,12},{1,5},{5,9},{9,13},{2,6},{6,10},{10,14},{3,7},{... | collective-permute-start | bytes 96776 | tf_op jit(solution)/shard_map/ppermute | solution.py:30
  78.0 3.7 %copy-start.30 = (f32[16,8,256]{2,1,0:T(8,128)S(1)}, f32[16,8,256]{2,1,0:T(8,128)}, u32[]{:S(2)}) copy-start(f32[16,8,256]{2,1,0:T(8,128)} %copy-done.29) | copy-start | bytes 393220
  78.0 3.7 %copy-start.32 = (f32[16,8,256]{2,1,0:T(8,128)S(1)}, f32[16,8,256]{2,1,0:T(8,128)}, u32[]{:S(2)}) copy-start(f32[16,8,256]{2,1,0:T(8,128)} %copy-done.31) | copy-start | bytes 393220
  78.1 3.7 %copy-start.34 = (f32[16,8,256]{2,1,0:T(8,128)S(1)}, f32[16,8,256]{2,1,0:T(8,128)}, u32[]{:S(2)}) copy-start(f32[16,8,256]{2,1,0:T(8,128)} %copy-done.33) | copy-start | bytes 393220
  78.1 3.7 %copy-start.36 = (f32[16,8,256]{2,1,0:T(8,128)S(1)}, f32[16,8,256]{2,1,0:T(8,128)}, u32[]{:S(2)}) copy-start(f32[16,8,256]{2,1,0:T(8,128)} %copy-done.35) | copy-start | bytes 393220
  78.1 3.7 %copy-start.38 = (f32[16,8,256]{2,1,0:T(8,128)S(1)}, f32[16,8,256]{2,1,0:T(8,128)}, u32[]{:S(2)}) copy-start(f32[16,8,256]{2,1,0:T(8,128)} %copy-done.37) | copy-start | bytes 393220
  86.8 20.7 %copy-start = (f32[16,8,256]{2,1,0:T(8,128)S(1)}, f32[16,8,256]{2,1,0:T(8,128)}, u32[]{:S(2)}) copy-start(f32[16,8,256]{2,1,0:T(8,128)} %get-tuple-element.116) | copy-start | bytes 393220
  86.8 21.6 %copy-start.62 = (f32[1,16,8,256]{3,2,1,0:T(8,128)S(1)}, f32[1,16,8,256]{3,2,1,0:T(8,128)}, u32[]{:S(2)}) copy-start(f32[1,16,8,256]{3,2,1,0:T(8,128)} %get-tuple-element.32) | copy-start | bytes 393220
  86.8 21.6 %copy-start.72 = (s32[256]{0:T(256)S(1)}, s32[256]{0:T(256)}, u32[]{:S(2)}) copy-start(s32[256]{0:T(256)} %copy-done.69) | copy-start | bytes 3076
  86.8 21.7 %copy-start.76 = (s32[256]{0:T(256)S(1)}, s32[256]{0:T(256)}, u32[]{:S(2)}) copy-start(s32[256]{0:T(256)} %copy-done.73) | copy-start | bytes 3076
  86.8 21.7 %copy-start.80 = (s32[256]{0:T(256)S(1)}, s32[256]{0:T(256)}, u32[]{:S(2)}) copy-start(s32[256]{0:T(256)} %copy-done.77) | copy-start | bytes 3076
  86.8 21.7 %copy-start.84 = (s32[256]{0:T(256)S(1)}, s32[256]{0:T(256)}, u32[]{:S(2)}) copy-start(s32[256]{0:T(256)} %copy-done.81) | copy-start | bytes 3076
  87.0 21.5 %copy-start.58 = (f32[3,16,8,256]{3,2,1,0:T(8,128)S(1)}, f32[3,16,8,256]{3,2,1,0:T(8,128)}, u32[]{:S(2)}) copy-start(f32[3,16,8,256]{3,2,1,0:T(8,128)} %get-tuple-element.167) | copy-start | bytes 1179652
  116.1 21.0 %collective-permute-start.5 = (f32[1,3,3,7,128]{4,2,3,1,0:T(4,128)S(1)}, f32[1,3,3,7,128]{4,2,3,1,0:T(4,128)S(1)}, u32[]{:S(2)}, u32[]{:S(2)}) collective-permute-start(f32[1,3,3,7,128]{4,2,3,1,0:T(4,128)S(1)} %slice.1059), channel_id=1, source_target_pairs={{0,4},{4,8},{8,12},{1,5},{5,9},{9,13},{2,6},{6,10},{10,14},{3,7},{... | collective-permute-start | bytes 96776 | tf_op jit(solution)/shard_map/ppermute | solution.py:30
  (125 other events, 157.0 us)
Sparse Core Ops, SparseCore 0:
  85.9 21.5 all-reduce.3
where the time goes:
time: 161 us; the launch traced here: 160 us
  blocking collectives  69.6 us (43%)
  waiting for transfers between devices  20.7 us (13%)
  between operations  17.3 us (11%)
  starting transfers between devices  16.8 us (10%)
  other arithmetic  16.6 us (10%)
  local copies, waits for them, and re-layouts  11.8 us (7%)
  matrix products  7.5 us (5%)
    psum x2, blocking collectives, from_root(): return lax.psum(kept, axis)  35.2 us
    all_gather x2, blocking collectives, shards(): lax.all_gather(head_rows.astype(jnp.bfloat16), 'slab', axis=2, tiled=True)  26.7 us
    psum x1, waiting for transfers between devices, shards(): current = lax.psum(warped, 'subj') / cohort  20.5 us
    unnamed x283, local copies, waits for them, and re-layouts  8.37 us
    psum x2, blocking collectives, shards(): lax.psum(band_grid.astype(jnp.bfloat16), 'yslab').astype(jnp.float32)  7.77 us
    ppermute x2, starting transfers between devices, shifted(): return lax.ppermute(block, axis, route)  7.15 us
    ppermute x2, starting transfers between devices, extended_2(): before = lax.ppermute(last, axis, up)  7.04 us
    another operation x6, other arithmetic, trilinear_local(): return (warped, jnp.stack([slope_z, slope_y, slope_x]))  6.89 us
  transfers between devices with their start and end apart: 7, of which 2 were waited for; matrix products, arithmetic and copies ran while one was open for 2% of the time, Pallas kernels for 0%

commit v1 on v0

--- a/solution.py
+++ b/solution.py
@@ -32,7 +32,7 @@
 
 def from_root(value, axis, source):
     kept = jnp.where(lax.axis_index(axis) == source, value, 0).astype(value.dtype)
-    return lax.psum(kept, axis)
+    return jnp.sum(lax.all_gather(kept, axis), axis=0)
 
 
 def basis(positions, columns, spacing, wrap):

time: 161 us -> 155 us (0.963)
  blocking collectives: 69.6 us -> 61.4 us
    psum x2 -> x0, blocking collectives: 35.2 us -> none  [from_root(): return lax.psum(kept, axis)]
    all_gather x0 -> x2, blocking collectives: none -> 26.9 us  [from_root(): return jnp.sum(lax.all_gather(kept, axis), axis=0)]
    unnamed x283 -> x289, local copies, waits for them, and re-layouts: 8.37 us -> 8.64 us
where the time goes in v1:
time: 155 us; the launch traced here: 154 us
  blocking collectives  61.4 us (40%)
  waiting for transfers between devices  21.8 us (14%)
  between operations  17.4 us (11%)
  starting transfers between devices  16.8 us (11%)
  other arithmetic  16.7 us (11%)
  local copies, waits for them, and re-layouts  12.1 us (8%)
  matrix products  7.96 us (5%)
    all_gather x2, blocking collectives, from_root(): return jnp.sum(lax.all_gather(kept, axis), axis=0)  26.9 us
    all_gather x2, blocking collectives, shards(): lax.all_gather(head_rows.astype(jnp.bfloat16), 'slab', axis=2, tiled=True)  26.8 us
    psum x1, waiting for transfers between devices, shards(): current = lax.psum(warped, 'subj') / cohort  21.6 us
    unnamed x289, local copies, waits for them, and re-layouts  8.64 us
    psum x2, blocking collectives, shards(): lax.psum(band_grid.astype(jnp.bfloat16), 'yslab').astype(jnp.float32)  7.77 us
    ppermute x2, starting transfers between devices, shifted(): return lax.ppermute(block, axis, route)  7.15 us
    ppermute x2, starting transfers between devices, extended_2(): before = lax.ppermute(last, axis, up)  7.04 us
    another operation x6, other arithmetic, trilinear_local(): return (warped, jnp.stack([slope_z, slope_y, slope_x]))  6.94 us
  transfers between devices with their start and end apart: 7, of which 2 were waited for; matrix products, arithmetic and copies ran while one was open for 2% of the time, Pallas kernels for 0%

profile of v1, /device:TPU:0, one launch (start us, length us, event | category | flops | bytes accessed | tf_op | source)
XLA Modules:
  0.0 154.2 jit_solution(13176367162725013996)
XLA Ops:
  7.9 1.3 collective-permute-start.1
  9.2 5.6 %collective-permute-start = (bf16[1,2,8,256]{3,2,1,0:T(8,128)(2,1)S(1)}, bf16[1,2,8,256]{3,2,1,0:T(8,128)(2,1)S(1)}, u32[]{:S(2)}, u32[]{:S(2)}) collective-permute-start(bf16[1,2,8,256]{3,2,1,0:T(8,128)(2,1)S(1)} %get-tuple-element.164), channel_id=1, source_target_pairs={{0,4},{4,8},{8,12},{1,5},{5,9},{9,13},{2,6},{6,10},{10,14},{3,7},{... | collective-permute-start | bytes 24584 | tf_op jit(solution)/shard_map/ppermute | solution.py:21
  15.2 0.9 constant_dynamic-slice_fusion.1
  17.6 1.5 collective-permute-start.2
  19.0 1.3 collective-permute-start.3
  20.4 1.5 %multiply_add_fusion.1 = (f32[3,16,8,256]{3,2,1,0:T(8,128)S(1)}, f32[3,16,8,256]{3,2,1,0:T(8,128)}) fusion(f32[3,16,8,128]{3,2,1,0:T(8,128)S(1)} %convolution_bitcast_fusion.3, f32[256]{0:T(256)S(1)} %get-tuple-element.193, s32[256]{0:T(256)S(1)} %get-tuple-element.186, f32[256]{0:T(256)S(1)} %get-tuple-element.192, s32[256]{0:T(256)S(1)} %get-tuple-element.187, ...), kind=kOutput, calls=%fused_computation.34 | convolution fusion | flops 151552000 | bytes 991232 | tf_op jit(solution)/shard_map/czyg,xg->czyx/dot_general | solution.py:63
  25.5 3.3 %fusion.332 = (f32[16,8,256]{2,1,0:T(8,128)S(1)}, f32[16,8,256]{2,1,0:T(8,128)}, f32[16,8,256]{2,1,0:T(8,128)S(1)}, f32[16,8,256]{2,1,0:T(8,128)S(1)}, f32[16,8,...) fusion(f32[16,8,256]{2,1,0:T(8,128)S(1)} %copy-done.63, ...), kind=kLoop, calls=%fused_computation.597 | loop fusion | flops 8093696 | bytes 21266432 | tf_op jit(solution)/shard_map/sub | solution.py:137
  30.5 2.9 %add_bitcast_fusion.2 = (f32[1,16,8,256]{3,2,1,0:T(8,128)S(1)}, f32[16,8,256]{2,1,0:T(8,128)}, f32[16,8,256]{2,1,0:T(8,128)}, f32[16,8,256]{2,1,0:T(8,128)}, f32...) fusion(pred[1,1,16,8,256]{4,3,2,1,0:T(8,128)(4,1)S(1)} %get-tup, ...), kind=kLoop, calls=%fused_computation.248 | loop fusion | flops 2654208 | bytes 8454144 | tf_op jit(solution)/shard_map/stack | solution.py:114
  34.1 0.8 fusion.4
  35.9 4.3 %psum.28 = bf16[1,3,7,7,128]{4,2,3,1,0:T(8,128)(2,1)S(1)} all-reduce(bf16[1,3,7,7,128]{4,2,3,1,0:T(8,128)(2,1)S(1)} %fusion), channel_id=1, replica_groups=mesh['group'=2,'slab'=4,'subj'=2,'yslab'=2] {'yslab'}, use_global_device_ids=true, to_apply=%region_0.1 | all-reduce | flops 18816 | bytes 75264 | tf_op jit(solution)/shard_map/psum | solution.py:142
  40.9 3.8 %collective-permute-start.4 = (f32[1,3,3,7,128]{4,2,3,1,0:T(4,128)S(1)}, f32[1,3,3,7,128]{4,2,3,1,0:T(4,128)S(1)}, u32[]{:S(2)}, u32[]{:S(2)}) collective-permute-start(f32[1,3,3,7,128]{4,2,3,1,0:T(4,128)S(1)} %slice.1053), channel_id=1, source_target_pairs={{0,4},{4,8},{8,12},{1,5},{5,9},{9,13},{2,6},{6,10},{10,14},{3,7},{... | collective-permute-start | bytes 96776 | tf_op jit(solution)/shard_map/ppermute | solution.py:30
  44.6 13.4 %all-gather = f32[4,3,3,7,128]{4,3,2,1,0:T(8,128)S(1)} all-gather(f32[1,3,3,7,128]{4,3,2,1,0:T(8,128)S(1)} %copy.21), channel_id=2, replica_groups=mesh['group'=2,'slab'=4,'subj'=2,'yslab'=2] {'slab'}, dimensions={0}, use_global_device_ids=true | all-gather | bytes 161280 | tf_op jit(solution)/shard_map/all_gather | solution.py:35
  59.0 13.4 %all_gather.18 = bf16[1,3,16,7,128]{4,3,1,0,2:T(8,128)(2,1)S(1)} all-gather(bf16[1,3,4,7,128]{4,3,1,0,2:T(8,128)(2,1)S(1)} %copy.20), channel_id=1, replica_groups=mesh['group'=2,'slab'=4,'subj'=2,'yslab'=2] {'slab'}, dimensions={2}, use_global_device_ids=true | all-gather | bytes 107520 | tf_op jit(solution)/shard_map/all_gather | solution.py:147
  74.1 1.1 copy_subtract_fusion
  75.3 1.1 convolution_bitcast_fusion.4
  76.9 1.5 %multiply_add_fusion = (f32[3,16,8,256]{3,2,1,0:T(8,128)S(1)}, f32[3,16,8,256]{3,2,1,0:T(8,128)}) fusion(f32[3,16,8,128]{3,2,1,0:T(8,128)S(1)} %convolution_bitcast_fusion.1, f32[256]{0:T(256)S(1)} %get-tuple-element.193, s32[256]{0:T(256)S(1)} %copy-done.78, f32[256]{0:T(256)S(1)} %get-tuple-element.192, s32[256]{0:T(256)S(1)} %copy-done.82, ...), kind=kOutput, calls=%fused_computation.31 | convolution fusion | flops 151552000 | bytes 991232 | tf_op jit(solution)/shard_map/czyg,xg->czyx/dot_general | solution.py:63
  78.6 3.0 %subtract_bitcast_fusion = (f32[1,16,8,256]{3,2,1,0:T(8,128)}, f32[16,8,256]{2,1,0:T(8,128)S(1)}, f32[16,8,256]{2,1,0:T(8,128)S(1)}, f32[16,8,256]{2,1,0:T(8,128...) fusion(pred[1,1,16,8,256]{4,3,2,1,0:T(8,128)(4,1)S(1)} %get-tup, ...), kind=kLoop, calls=%fused_computation.191 | loop fusion | flops 4227072 | bytes 8716288 | tf_op jit(solution)/shard_map/stack | solution.py:114
  83.7 21.6 %all-reduce.4.cloned.1.call-done = (f32[16,8,256]{2,1,0:T(8,128)}, f32[16,8,256]{2,1,0:T(8,128)}) async-done(((f32[16,8,256]{2,1,0:T(8,128)}, f32[16,8,256]{2,1,0:T(8,128)}), (f32[16,8,256]{2,1,0:T(8,128)}, f32[16,8,256]{2,1,0:T(8,128)})) %all-reduce.4.cloned.1.call-update) | async-done | bytes 262160 | tf_op jit(solution)/shard_map/psum | solution.py:141
  105.3 0.9 multiply_subtract_fusion
  108.8 3.5 %psum.31 = bf16[1,3,7,7,128]{4,2,3,1,0:T(8,128)(2,1)S(1)} all-reduce(bf16[1,3,7,7,128]{4,2,3,1,0:T(8,128)(2,1)S(1)} %fusion.1), channel_id=1, replica_groups=mesh['group'=2,'slab'=4,'subj'=2,'yslab'=2] {'yslab'}, use_global_device_ids=true, to_apply=%region_6.7 | all-reduce | flops 18816 | bytes 75264 | tf_op jit(solution)/shard_map/psum | solution.py:142
  114.0 3.4 %collective-permute-start.5 = (f32[1,3,3,7,128]{4,2,3,1,0:T(4,128)S(1)}, f32[1,3,3,7,128]{4,2,3,1,0:T(4,128)S(1)}, u32[]{:S(2)}, u32[]{:S(2)}) collective-permute-start(f32[1,3,3,7,128]{4,2,3,1,0:T(4,128)S(1)} %slice.1059), channel_id=1, source_target_pairs={{0,4},{4,8},{8,12},{1,5},{5,9},{9,13},{2,6},{6,10},{10,14},{3,7},{... | collective-permute-start | bytes 96776 | tf_op jit(solution)/shard_map/ppermute | solution.py:30
  117.4 13.4 %all-gather.1 = f32[4,3,3,7,128]{4,3,2,1,0:T(8,128)S(1)} all-gather(f32[1,3,3,7,128]{4,3,2,1,0:T(8,128)S(1)} %copy.30), channel_id=3, replica_groups=mesh['group'=2,'slab'=4,'subj'=2,'yslab'=2] {'slab'}, dimensions={0}, use_global_device_ids=true | all-gather | bytes 161280 | tf_op jit(solution)/shard_map/all_gather | solution.py:35
  131.7 13.3 %all_gather.21 = bf16[1,3,16,7,128]{4,3,1,0,2:T(8,128)(2,1)S(1)} all-gather(bf16[1,3,4,7,128]{4,3,1,0,2:T(8,128)(2,1)S(1)} %copy.29), channel_id=1, replica_groups=mesh['group'=2,'slab'=4,'subj'=2,'yslab'=2] {'slab'}, dimensions={2}, use_global_device_ids=true | all-gather | bytes 107520 | tf_op jit(solution)/shard_map/all_gather | solution.py:147
  146.4 0.9 copy.33
  (360 shorter events, 19.1 us)
Async XLA Ops:
  7.2 98.1 %all-reduce.4.cloned.1.call-start = ((), (), s32[]{:S(2)}) async-start(), calls=%async_computation | async-start | bytes 524288 | tf_op jit(solution)/shard_map/psum | solution.py:141
  7.9 9.6 %collective-permute-start.1 = (bf16[1,2,8,256]{3,2,1,0:T(8,128)(2,1)S(1)}, bf16[1,2,8,256]{3,2,1,0:T(8,128)(2,1)S(1)}, u32[]{:S(2)}, u32[]{:S(2)}) collective-permute-start(bf16[1,2,8,256]{3,2,1,0:T(8,128)(2,1)S(1)} %get-tuple-element.163), channel_id=1, source_target_pairs={{4,0},{8,4},{12,8},{5,1},{9,5},{13,9},{6,2},{10,6},{14,10},{7,3},{... | collective-permute-start | bytes 24584 | tf_op jit(solution)/shard_map/ppermute | solution.py:22
  9.2 7.9 %collective-permute-start = (bf16[1,2,8,256]{3,2,1,0:T(8,128)(2,1)S(1)}, bf16[1,2,8,256]{3,2,1,0:T(8,128)(2,1)S(1)}, u32[]{:S(2)}, u32[]{:S(2)}) collective-permute-start(bf16[1,2,8,256]{3,2,1,0:T(8,128)(2,1)S(1)} %get-tuple-element.164), channel_id=1, source_target_pairs={{0,4},{4,8},{8,12},{1,5},{5,9},{9,13},{2,6},{6,10},{10,14},{3,7},{... | collective-permute-start | bytes 24584 | tf_op jit(solution)/shard_map/ppermute | solution.py:21
  15.1 18.3 %copy-start.65 = (f32[256]{0:T(256)}, f32[256]{0:T(256)S(1)}, u32[]{:S(2)}) copy-start(f32[256]{0:T(256)S(1)} %get-tuple-element.191) | copy-start | bytes 3076
  15.2 5.2 %copy-start.68 = (s32[256]{0:T(256)}, s32[256]{0:T(256)S(1)}, u32[]{:S(2)}) copy-start(s32[256]{0:T(256)S(1)} %get-tuple-element.188) | copy-start | bytes 3076
  15.2 5.2 %copy-start.72 = (s32[256]{0:T(256)}, s32[256]{0:T(256)S(1)}, u32[]{:S(2)}) copy-start(s32[256]{0:T(256)S(1)} %get-tuple-element.189) | copy-start | bytes 3076
  17.6 4.4 %collective-permute-start.2 = (bf16[1,20,2,256]{3,2,1,0:T(2,128)(2,1)S(1)}, bf16[1,20,2,256]{3,2,1,0:T(2,128)(2,1)S(1)}, u32[]{:S(2)}, u32[]{:S(2)}) collective-permute-start(bf16[1,20,2,256]{3,2,1,0:T(2,128)(2,1)S(1)} %get-tuple-element.161), channel_id=1, source_target_pairs={{0,1},{2,3},{4,5},{6,7},{8,9},{10,11},{12,13},{14,15},{16,17},{18,... | collective-permute-start | bytes 61448 | tf_op jit(solution)/shard_map/ppermute | solution.py:21
  19.0 3.1 %collective-permute-start.3 = (bf16[1,20,2,256]{3,2,1,0:T(2,128)(2,1)S(1)}, bf16[1,20,2,256]{3,2,1,0:T(2,128)(2,1)S(1)}, u32[]{:S(2)}, u32[]{:S(2)}) collective-permute-start(bf16[1,20,2,256]{3,2,1,0:T(2,128)(2,1)S(1)} %get-tuple-element.162), channel_id=1, source_target_pairs={{1,0},{3,2},{5,4},{7,6},{9,8},{11,10},{13,12},{15,14},{17,16},{19,... | collective-permute-start | bytes 61448 | tf_op jit(solution)/shard_map/ppermute | solution.py:22
  40.9 17.2 %collective-permute-start.4 = (f32[1,3,3,7,128]{4,2,3,1,0:T(4,128)S(1)}, f32[1,3,3,7,128]{4,2,3,1,0:T(4,128)S(1)}, u32[]{:S(2)}, u32[]{:S(2)}) collective-permute-start(f32[1,3,3,7,128]{4,2,3,1,0:T(4,128)S(1)} %slice.1053), channel_id=1, source_target_pairs={{0,4},{4,8},{8,12},{1,5},{5,9},{9,13},{2,6},{6,10},{10,14},{3,7},{... | collective-permute-start | bytes 96776 | tf_op jit(solution)/shard_map/ppermute | solution.py:30
  72.4 3.9 %copy-start.106 = (f32[8]{0:T(128)S(1)}, f32[8]{0:T(128)}, u32[]{:S(2)}) copy-start(f32[8]{0:T(128)} %copy-done.104) | copy-start | bytes 100
  74.0 4.5 %copy-start.28 = (f32[16,8,256]{2,1,0:T(8,128)S(1)}, f32[16,8,256]{2,1,0:T(8,128)}, u32[]{:S(2)}) copy-start(f32[16,8,256]{2,1,0:T(8,128)} %copy-done.27) | copy-start | bytes 393220
  74.0 4.5 %copy-start.30 = (f32[16,8,256]{2,1,0:T(8,128)S(1)}, f32[16,8,256]{2,1,0:T(8,128)}, u32[]{:S(2)}) copy-start(f32[16,8,256]{2,1,0:T(8,128)} %copy-done.29) | copy-start | bytes 393220
  74.0 4.5 %copy-start.32 = (f32[16,8,256]{2,1,0:T(8,128)S(1)}, f32[16,8,256]{2,1,0:T(8,128)}, u32[]{:S(2)}) copy-start(f32[16,8,256]{2,1,0:T(8,128)} %copy-done.31) | copy-start | bytes 393220
  74.0 4.5 %copy-start.34 = (f32[16,8,256]{2,1,0:T(8,128)S(1)}, f32[16,8,256]{2,1,0:T(8,128)}, u32[]{:S(2)}) copy-start(f32[16,8,256]{2,1,0:T(8,128)} %copy-done.33) | copy-start | bytes 393220
  74.0 4.5 %copy-start.36 = (f32[16,8,256]{2,1,0:T(8,128)S(1)}, f32[16,8,256]{2,1,0:T(8,128)}, u32[]{:S(2)}) copy-start(f32[16,8,256]{2,1,0:T(8,128)} %copy-done.35) | copy-start | bytes 393220
  74.0 4.5 %copy-start.38 = (f32[16,8,256]{2,1,0:T(8,128)S(1)}, f32[16,8,256]{2,1,0:T(8,128)}, u32[]{:S(2)}) copy-start(f32[16,8,256]{2,1,0:T(8,128)} %copy-done.37) | copy-start | bytes 393220
  83.5 21.8 %copy-start = (f32[16,8,256]{2,1,0:T(8,128)S(1)}, f32[16,8,256]{2,1,0:T(8,128)}, u32[]{:S(2)}) copy-start(f32[16,8,256]{2,1,0:T(8,128)} %get-tuple-element.118) | copy-start | bytes 393220
  83.5 22.7 %copy-start.61 = (f32[1,16,8,256]{3,2,1,0:T(8,128)S(1)}, f32[1,16,8,256]{3,2,1,0:T(8,128)}, u32[]{:S(2)}) copy-start(f32[1,16,8,256]{3,2,1,0:T(8,128)} %get-tuple-element.34) | copy-start | bytes 393220
  83.5 22.7 %copy-start.71 = (s32[256]{0:T(256)S(1)}, s32[256]{0:T(256)}, u32[]{:S(2)}) copy-start(s32[256]{0:T(256)} %copy-done.68) | copy-start | bytes 3076
  83.5 22.8 %copy-start.75 = (s32[256]{0:T(256)S(1)}, s32[256]{0:T(256)}, u32[]{:S(2)}) copy-start(s32[256]{0:T(256)} %copy-done.72) | copy-start | bytes 3076
  83.5 22.8 %copy-start.79 = (s32[256]{0:T(256)S(1)}, s32[256]{0:T(256)}, u32[]{:S(2)}) copy-start(s32[256]{0:T(256)} %copy-done.76) | copy-start | bytes 3076
  83.5 22.8 %copy-start.83 = (s32[256]{0:T(256)S(1)}, s32[256]{0:T(256)}, u32[]{:S(2)}) copy-start(s32[256]{0:T(256)} %copy-done.80) | copy-start | bytes 3076
  83.7 22.6 %copy-start.58 = (f32[3,16,8,256]{3,2,1,0:T(8,128)S(1)}, f32[3,16,8,256]{3,2,1,0:T(8,128)}, u32[]{:S(2)}) copy-start(f32[3,16,8,256]{3,2,1,0:T(8,128)} %get-tuple-element.169) | copy-start | bytes 1179652
  114.0 16.9 %collective-permute-start.5 = (f32[1,3,3,7,128]{4,2,3,1,0:T(4,128)S(1)}, f32[1,3,3,7,128]{4,2,3,1,0:T(4,128)S(1)}, u32[]{:S(2)}, u32[]{:S(2)}) collective-permute-start(f32[1,3,3,7,128]{4,2,3,1,0:T(4,128)S(1)} %slice.1059), channel_id=1, source_target_pairs={{0,4},{4,8},{8,12},{1,5},{5,9},{9,13},{2,6},{6,10},{10,14},{3,7},{... | collective-permute-start | bytes 96776 | tf_op jit(solution)/shard_map/ppermute | solution.py:30
  (128 other events, 181.9 us)
Sparse Core Ops, SparseCore 0:
  82.6 22.6 all-reduce.3
